TPU v7x, 128 devices: a whole 4x4x4 slice. The times are simulated.
128 devices in a mesh: leaf: 128 (over y, z, x, core).
Axes of the slice: x: 4, y: 4, z: 4, core: 2. Of those that a mesh axis runs over, the one named last changes fastest.
Arguments:
- density: bfloat16 [131072, 220], P('leaf'), may hold values from -6 to 6
- vel_mask: int32 [131072], P('leaf'), may hold values from 0 to 1, as said below
- near_list: int32 [131072, 27], P('leaf'), may hold values from 0 to 131071, as said below
- near_ops: bfloat16 [27, 220, 660], replicated, may hold values from -0.078125 to 0.078125
- upward_ops: bfloat16 [8, 220, 56], replicated, may hold values from -0.0068359375 to 0.0068359375
- coupling_operators: float32 [56, 168], replicated, may hold values from -0.75 to 0.75
- coarse_weights: float32 [32, 32], replicated, may hold values from -1 to 1
- downward_ops: bfloat16 [8, 56, 220], replicated, may hold values from -0.75 to 0.75
- conc_owner: int32 [131072, 1], P('leaf'), may hold values from 0 to 127; in each aligned block of 1024 rows (0 to 1023, 1024 to 2047, ...) at most 16 rows name the same one
- concentration: bfloat16 [262144, 220], P('leaf'), may hold values from -6 to 6
- departure: int32 [262144], P('leaf'), may hold values from 0 to 2047
- departure_class: int32 [262144], P('leaf'), may hold values from 0 to 7
- shift_ops: bfloat16 [8, 220, 220], replicated, may hold values from -0.4375 to 0.4375
- eval_ops: bfloat16 [220, 1024], replicated, may hold values from -0.4375 to 0.4375
Outputs:
- velocity: bfloat16 [131072, 660], P('leaf')
- advected: bfloat16 [262144, 256], P('leaf')
Inputs may be any that keep to these rules, and one draw needn't show every extreme that they name: `vel_mask`: in each aligned block of 1024 rows the real leaves come first; every block has from 341 to 1024 real leaves, and both counts occur in every draw. `near_list`: entry [i, t] lies within 1024 of i; column 13 is i itself. `conc_owner`: in each aligned block of 1024 rows, the rows of one device, no owner is named more than 16 times, a bound that some block reaches. `departure`: A slot index within the same device's 2048 slots.
All inputs are finite; a program needn't handle non-finite values.
Results may differ from a plain program's by a relative error of at most 0.008.
Values may be sent and summed in bfloat16 or wider, within the bound.
No kernel may reach another device: no remote copies, remote signals or barrier semaphores. Data moves between devices by JAX's collectives and lax.ppermute only.
A program may use at most 128 MiB of HBM per device.

v0:
```python
import jax
import jax.numpy as jnp
from jax import lax
from jax.sharding import PartitionSpec as P

SPAN = 4


time_step = 0.5


def with_halo(block, sides, width):
    for axis, dim in sides:
        count = lax.axis_size(axis)
        forward = [(i, i + 1) for i in range(count - 1)]
        backward = [(target, source) for source, target in forward]
        low = lax.ppermute(
            lax.slice_in_dim(block, block.shape[dim] - width, None, axis=dim), axis, forward
        )
        high = lax.ppermute(lax.slice_in_dim(block, 0, width, axis=dim), axis, backward)
        block = jnp.concatenate([low, block, high], axis=dim)
    return block


def shifted_rows(gathered, classes, shift_ops):
    kinds = shift_ops.shape[0]
    total = jnp.zeros((gathered.shape[0], shift_ops.shape[2]), jnp.float32)
    for kind in range(kinds):
        product = jnp.dot(gathered, shift_ops[kind], preferred_element_type=jnp.float32)
        total = jnp.where((classes == kind)[:, None], product, total)
    return total.astype(jnp.bfloat16)


def advect_rows(base, velocity_rows, alive_rows, eval_ops):
    value_rows = jnp.dot(base, eval_ops, preferred_element_type=jnp.float32)
    nodes_count = value_rows.shape[1] // 4
    speeds = jnp.dot(
        velocity_rows.reshape(-1, eval_ops.shape[0]),
        eval_ops[:, :nodes_count],
        preferred_element_type=jnp.float32,
    )
    speeds = speeds.reshape(base.shape[0], 3, nodes_count)
    correction = speeds[:, 0] * value_rows[:, nodes_count : 2 * nodes_count]
    correction = correction + speeds[:, 1] * value_rows[:, 2 * nodes_count : 3 * nodes_count]
    correction = correction + speeds[:, 2] * value_rows[:, 3 * nodes_count :]
    return (alive_rows[:, None] * (value_rows[:, :nodes_count] - time_step * correction)).astype(
        jnp.bfloat16
    )


def local(
    density,
    vel_mask,
    near_list,
    near_ops,
    upward_ops,
    coupling_operators,
    coarse_weights,
    downward_ops,
    conc_owner,
    concentration,
    departure,
    departure_class,
    shift_ops,
    eval_ops,
):
    leaves = density.shape[0]
    coef_width = density.shape[1]
    devices = lax.axis_size("leaf")
    my_index = lax.axis_index("leaf")
    alive = vel_mask.astype(jnp.float32)
    live_density = (density.astype(jnp.float32) * alive[:, None]).astype(jnp.bfloat16)
    padded = with_halo(live_density, (("leaf", 0),), leaves)
    local_rows = near_list - my_index * leaves + leaves

    def near_step(position, total):
        rows = lax.dynamic_index_in_dim(local_rows, position, 1, keepdims=False)
        picked = jnp.take(padded, rows, axis=0)
        operator = lax.dynamic_index_in_dim(near_ops, position, 0, keepdims=False)
        return total + jnp.dot(picked, operator, preferred_element_type=jnp.float32)

    nearby_field = lax.fori_loop(
        0, near_ops.shape[0], near_step, jnp.zeros((leaves, 3 * coef_width), jnp.float32)
    )
    parts = jnp.einsum(
        "gop,opq->goq",
        live_density.reshape(-1, 8, coef_width),
        upward_ops,
        preferred_element_type=jnp.float32,
    )
    own_part = jnp.sum(parts, axis=(0, 1))
    boxes = devices // SPAN
    my_box = my_index // SPAN
    box_rows = (jnp.arange(boxes, dtype=jnp.int32) == my_box).astype(jnp.float32)
    moments = lax.psum(box_rows[:, None] * own_part[None, :], "leaf")
    expanded = jnp.dot(moments, coupling_operators, precision=lax.Precision.HIGHEST)
    weight_row = lax.dynamic_slice_in_dim(coarse_weights, my_box, 1, 0)
    own_expansion = jnp.dot(weight_row, expanded, precision=lax.Precision.HIGHEST)
    box_far = jnp.einsum(
        "jq,oqp->ojp",
        own_expansion.reshape(3, -1),
        downward_ops.astype(jnp.float32),
        precision=lax.Precision.HIGHEST,
    )
    far_field = jnp.broadcast_to(
        box_far.reshape(1, 8, 3 * coef_width), (leaves // 8, 8, 3 * coef_width)
    ).reshape(leaves, 3 * coef_width)
    velocity = ((nearby_field + far_field) * alive[:, None]).astype(jnp.bfloat16)
    slots_here = concentration.shape[0]
    capacity = slots_here // devices
    owner = conc_owner[:, 0]
    onehot = (owner[:, None] == jnp.arange(devices, dtype=jnp.int32)[None, :]).astype(jnp.int32)
    rank = jnp.sum(jnp.cumsum(onehot, axis=0) * onehot, axis=1) - 1
    send_slot = owner * capacity + rank
    placement = (jnp.arange(slots_here, dtype=jnp.int32)[:, None] == send_slot[None, :]).astype(
        jnp.bfloat16
    )
    send_velocity = jnp.dot(placement, velocity, preferred_element_type=jnp.float32).astype(
        jnp.bfloat16
    )
    send_alive = jnp.dot(
        placement, vel_mask.astype(jnp.bfloat16), preferred_element_type=jnp.float32
    ).astype(jnp.bfloat16)
    got_velocity, got_alive = (
        lax.all_to_all(
            send_velocity.reshape(devices, capacity, -1),
            "leaf",
            split_axis=0,
            concat_axis=0,
            tiled=True,
        ),
        lax.all_to_all(
            send_alive.reshape(devices, capacity), "leaf", split_axis=0, concat_axis=0, tiled=True
        ),
    )
    base = shifted_rows(concentration[departure], departure_class, shift_ops)
    advected = advect_rows(
        base,
        got_velocity.reshape(slots_here, -1),
        got_alive.reshape(slots_here).astype(jnp.float32),
        eval_ops,
    )
    return (velocity, advected)


def solution(mesh):
    placed = (
        P("leaf", None),
        P("leaf"),
        P("leaf", None),
        P(),
        P(),
        P(),
        P(),
        P(),
        P("leaf", None),
        P("leaf", None),
        P("leaf"),
        P("leaf"),
        P(),
        P(),
    )
    return jax.shard_map(
        local,
        mesh=mesh,
        in_specs=placed,
        out_specs=(P("leaf", None), P("leaf", None)),
        check_vma=False,
    )
```

profile of v0, /device:TPU:1, one launch (start us, length us, event | category | flops | bytes accessed | tf_op | source)
XLA Modules:
  0.0 428.8 jit_solution(9726396116737616334)
XLA Ops:
  13.9 14.0 %all-to-all-start = ((bf16[128,1,16]{2,1,0:T(2,128)(2,1)}), bf16[128,1,16]{2,1,0:T(2,128)(2,1)S(1)}, u32[]{:S(2)}, u32[]{:S(2)}) async-start(bf16[128,1,16]{2,1,0:T(2,128)(2,1)} %all_to_all.12), calls=%async_computation | async-start | bytes 131072 | tf_op jit(solution)/shard_map/all_to_all | solution.py:132
  28.7 67.2 %psum.7 = f32[32,56]{1,0:T(8,128)S(1)} all-reduce(f32[32,56]{1,0:T(8,128)S(1)} %broadcast_multiply_fusion), channel_id=1, replica_groups=mesh['leaf'=128] {'leaf'}, use_global_device_ids=true, to_apply=%region_3.4 | all-reduce | flops 1792 | bytes 14336 | tf_op jit(solution)/shard_map/psum | solution.py:95
  99.5 7.5 %gather_fusion.1 = bf16[2048,220]{1,0:T(8,128)(2,1)S(1)} fusion(bf16[2048,220]{1,0:T(8,128)(2,1)S(1)} %copy.42, s32[2048]{0:T(1024)S(1)} %fusion.46), kind=kCustom, calls=%fused_computation.1 | custom fusion | bytes 1810432 | tf_op jit(solution)/shard_map/gather | solution.py:136
  111.1 237.2 %while.14 = (s32[]{:T(128)}, f32[1024,660]{0,1:T(8,128)}, s32[1024,27]{0,1:T(8,128)}, bf16[3072,220]{1,0:T(8,128)(2,1)S(1)}, bf16[27,220,660]{1,2,0:T(8,128)(2,1)}, /*index=5*/s32[]{:T(128)}, s32[]{:T(128)}) while((s32[]{:T(128)}, f32[1024,660]{0,1:T(8,128)}, s32[1024,27]{0,1:T(8,128)}, bf16[3072,220]{1,0:T(8,128)(2,1)S(1)}, ...), condition=%wide.region_1.2_spmd.clone, body=%wide.region_0.1_spmd.clone.sunk | while | flops 298953728 | bytes 7137383 | solution.py:82
  123.7 4.1 select_add_fusion.2
  141.4 4.1 select_add_fusion.2
  159.0 4.1 select_add_fusion.2
  176.6 4.1 select_add_fusion.2
  194.3 4.1 select_add_fusion.2
  211.9 4.1 select_add_fusion.2
  229.5 4.1 select_add_fusion.2
  247.2 4.1 select_add_fusion.2
  264.8 4.1 select_add_fusion.2
  282.4 4.1 select_add_fusion.2
  300.1 4.1 select_add_fusion.2
  317.7 4.1 select_add_fusion.2
  335.3 4.1 select_add_fusion.2
  353.9 4.5 %fusion.11 = bf16[2048,660]{0,1:T(8,128)(2,1)} fusion(bf16[1024,660]{1,0:T(8,128)(2,1)S(1)} %fusion.13, s32[1024]{0:T(1024)S(1)} %add_add_fusion), kind=kOutput, calls=%fused_computation.18 | convolution fusion | flops 2771689472 | bytes 4059136 | tf_op jit(solution)/shard_map/dot_general | solution.py:118
  358.3 4.6 %copy.51 = bf16[2048,660]{1,0:T(8,128)(2,1)} copy(bf16[2048,660]{0,1:T(8,128)(2,1)} %fusion.11) | data formatting | bytes 5406720 | tf_op jit(solution)/shard_map/convert_element_type | solution.py:118
  363.0 5.7 %all-to-all-start.1 = ((bf16[128,16,660]{2,1,0:T(8,128)(2,1)}), bf16[128,16,660]{2,1,0:T(8,128)(2,1)}, u32[]{:S(2)}, u32[]{:S(2)}) async-start(bf16[128,16,660]{2,1,0:T(8,128)(2,1)} %bitcast.102), calls=%async_computation.1 | async-start | bytes 6291456 | tf_op jit(solution)/shard_map/all_to_all | solution.py:125
  374.9 6.4 %fusion.28 = f32[2048,1024]{1,0:T(8,128)} fusion(bf16[220,1024]{1,0:T(8,128)(2,1)S(1)} %copy-done.4, bf16[2048,220]{0,1:T(8,128)(2,1)} %fusion.41, bf16[2048,220]{0,1:T(8,128)(2,1)} %fusion.19, bf16[2048,220]{1,0:T(8,128)(2,1)S(1)} %gather_fusion.1, pred[2048]{0:T(1024)(128)(4,1)S(1)} %get-tuple-element.144, pred[2048]{0:T(1024)(128)(4,1)S(1)} %get-tuple-element.139, ...), kind=kOutput, calls=%fused_computation.46 | convolution fusion | flops 1121894400 | bytes 11643424 | tf_op jit(solution)/shard_map/dot_general | solution.py:35
  383.1 27.0 %all-to-all-done.1 = bf16[128,16,660]{2,1,0:T(8,128)(2,1)} async-done(((bf16[128,16,660]{2,1,0:T(8,128)(2,1)}), bf16[128,16,660]{2,1,0:T(8,128)(2,1)}, u32[]{:S(2)}, u32[]{:S(2)}) %all-to-all-start.1) | async-done | bytes 2703392 | tf_op jit(solution)/shard_map/all_to_all | solution.py:125
  410.1 10.8 %dot_general.78 = bf16[2048,3,220]{2,1,0:T(4,128)(2,1)} reshape(bf16[128,16,660]{2,1,0:T(8,128)(2,1)} %all-to-all-done.1) | data formatting | bytes 5406720 | tf_op jit(solution)/shard_map/dot_general | solution.py:37
  424.1 4.6 %fusion.26 = bf16[2048,256]{1,0:T(8,128)(2,1)} fusion(f32[2048,1024]{1,0:T(8,128)} %fusion.28, f32[2048,3,256]{2,0,1:T(8,128)S(1)} %fusion.14, f32[2048]{0:T(1024)S(1)} %reshape.89), kind=kLoop, calls=%fused_computation.38 | loop fusion | flops 4718592 | bytes 15736832 | tf_op jit(solution)/shard_map/convert_element_type | solution.py:46
  (179 shorter events, 222.0 us)
Async XLA Ops:
  0.6 96.4 %copy-start = (bf16[8,56,220]{2,1,0:T(8,128)(2,1)S(1)}, bf16[8,56,220]{2,1,0:T(8,128)(2,1)}, u32[]{:S(2)}) copy-start(bf16[8,56,220]{2,1,0:T(8,128)(2,1)} %param.23) | copy-start | bytes 591364
  0.6 10.6 %copy-start.13 = (s32[1024,1]{0,1:T(1,128)S(1)}, s32[1024,1]{0,1:T(1,128)}, u32[]{:S(2)}) copy-start(s32[1024,1]{0,1:T(1,128)} %param.24) | copy-start | bytes 12292
  3.6 105.8 %collective-permute-start.1 = (bf16[1024,220]{1,0:T(8,128)(2,1)}, bf16[1024,220]{1,0:T(8,128)(2,1)}, u32[]{:S(2)}, u32[]{:S(2)}) collective-permute-start(bf16[1024,220]{1,0:T(8,128)(2,1)} %multiply_convert_fusion), channel_id=1, source_target_pairs={{1,0},{2,1},{3,2},{4,3},{5,4},{6,5},{7,6},{8,7},{9,8},{10,9},{11,1... | collective-permute-start | bytes 1351688 | tf_op jit(solution)/shard_map/ppermute | solution.py:20
  6.9 102.5 %collective-permute-start = (bf16[1024,220]{1,0:T(8,128)(2,1)}, bf16[1024,220]{1,0:T(8,128)(2,1)}, u32[]{:S(2)}, u32[]{:S(2)}) collective-permute-start(bf16[1024,220]{1,0:T(8,128)(2,1)} %multiply_convert_fusion), channel_id=1, source_target_pairs={{0,1},{1,2},{2,3},{3,4},{4,5},{5,6},{6,7},{7,8},{8,9},{9,10},{10,1... | collective-permute-start | bytes 1351688 | tf_op jit(solution)/shard_map/ppermute | solution.py:17
  11.3 16.9 %copy-start.15 = (s32[2048]{0:T(1024)S(1)}, s32[2048]{0:T(1024)}, u32[]{:S(2)}) copy-start(s32[2048]{0:T(1024)} %param.26) | copy-start | bytes 24580
  11.3 16.9 %copy-start.14 = (s32[2048]{0:T(1024)S(1)}, s32[2048]{0:T(1024)}, u32[]{:S(2)}) copy-start(s32[2048]{0:T(1024)} %param.27) | copy-start | bytes 24580
  11.3 16.9 %copy-start.16 = (bf16[8,220,56]{1,2,0:T(8,128)(2,1)S(1)}, bf16[8,220,56]{1,2,0:T(8,128)(2,1)}, u32[]{:S(2)}) copy-start(bf16[8,220,56]{1,2,0:T(8,128)(2,1)} %param.20) | copy-start | bytes 591364
  11.7 84.2 %copy-start.12 = (f32[56,168]{1,0:T(8,128)S(1)}, f32[56,168]{1,0:T(8,128)}, u32[]{:S(2)}) copy-start(f32[56,168]{1,0:T(8,128)} %param.21) | copy-start | bytes 112900
  11.7 85.7 %copy-start.3 = (bf16[2048,220]{0,1:T(8,128)(2,1)S(1)}, bf16[2048,220]{0,1:T(8,128)(2,1)}, u32[]{:S(2)}) copy-start(bf16[2048,220]{0,1:T(8,128)(2,1)} %param.25) | copy-start | bytes 2703364
  13.9 349.1 %all-to-all-start = ((bf16[128,1,16]{2,1,0:T(2,128)(2,1)}), bf16[128,1,16]{2,1,0:T(2,128)(2,1)S(1)}, u32[]{:S(2)}, u32[]{:S(2)}) async-start(bf16[128,1,16]{2,1,0:T(2,128)(2,1)} %all_to_all.12), calls=%async_computation | async-start | bytes 131072 | tf_op jit(solution)/shard_map/all_to_all | solution.py:132
  99.5 7.5 %copy-start.2 = (bf16[8,220,220]{2,0,1:T(8,128)(2,1)S(1)}, bf16[8,220,220]{2,0,1:T(8,128)(2,1)}, u32[]{:S(2)}) copy-start(bf16[8,220,220]{2,0,1:T(8,128)(2,1)} %param.28) | copy-start | bytes 2323204
  363.0 5.7 %copy-start.9 = (bf16[1,220,220]{2,0,1:T(2,128)(2,1)S(1)}, bf16[1,220,220]{2,0,1:T(2,128)(2,1)}, u32[]{:S(2)}) copy-start(bf16[1,220,220]{2,0,1:T(2,128)(2,1)} %get-tuple-element.132) | copy-start | bytes 290404
  363.0 6.2 %copy-start.8 = (bf16[1,220,220]{2,0,1:T(2,128)(2,1)S(1)}, bf16[1,220,220]{2,0,1:T(2,128)(2,1)}, u32[]{:S(2)}) copy-start(bf16[1,220,220]{2,0,1:T(2,128)(2,1)} %get-tuple-element.133) | copy-start | bytes 290404
  363.0 47.1 %all-to-all-start.1 = ((bf16[128,16,660]{2,1,0:T(8,128)(2,1)}), bf16[128,16,660]{2,1,0:T(8,128)(2,1)}, u32[]{:S(2)}, u32[]{:S(2)}) async-start(bf16[128,16,660]{2,1,0:T(8,128)(2,1)} %bitcast.102), calls=%async_computation.1 | async-start | bytes 6291456 | tf_op jit(solution)/shard_map/all_to_all | solution.py:125
  368.6 1.1 copy-start.7
  368.7 1.6 copy-start.6
  369.2 1.6 copy-start.5
  369.8 2.5 copy-start.11
  372.3 0.9 copy-start.10
  372.9 2.0 copy-start.4
  424.1 4.6 %copy-start.1 = (bf16[8,56,220]{2,1,0:T(8,128)(2,1)S(1)}, bf16[8,56,220]{2,1,0:T(8,128)(2,1)}, u32[]{:S(2)}) copy-start(bf16[8,56,220]{2,1,0:T(8,128)(2,1)} %param.23) | copy-start | bytes 591364
where the time goes:
time: 432 us; the launch traced here: 429 us
  local copies, waits for them, and re-layouts  141 us (33%)
  matrix products  132 us (31%)
  blocking collectives  67.2 us (16%)
  other arithmetic  34.3 us (8%)
  waiting for transfers between devices  27 us (6%)
  starting transfers between devices  26.1 us (6%)
    dot_general x27, matrix products, near_step(): return total + jnp.dot(picked, operator, preferred_element_type=jnp.float32)  109 us
    gather x27, local copies, waits for them, and re-layouts, near_step(): picked = jnp.take(padded, rows, axis=0)  106 us
    psum x1, blocking collectives, local(): moments = lax.psum(box_rows[:, None] * own_part[None, :], 'leaf')  67.2 us
    all_to_all x1, waiting for transfers between devices, local(): lax.all_to_all(send_velocity.reshape(devices, capacity, -1), 'leaf', spli...  27 us
    and x27, other arithmetic, near_step(): picked = jnp.take(padded, rows, axis=0)  21.3 us
    all_to_all x1, starting transfers between devices, local(): lax.all_to_all(send_alive.reshape(devices, capacity), 'leaf', split_axis=...  14 us
    dot_general x1, local copies, waits for them, and re-layouts, advect_rows(): jnp.dot(velocity_rows.reshape(-1, eval_ops.shape[0]), eval_ops[:, :nodes_...  10.8 us
  transfers between devices with their start and end apart: 4, of which 1 were waited for; matrix products, arithmetic and copies ran while one was open for 66% of the time, Pallas kernels for 0%

commit v1 on v0

v1 whole, which is shorter than its diff:
```python
import jax
import jax.numpy as jnp
from jax import lax
from jax.experimental import pallas as pl
from jax.experimental.pallas import tpu as pltpu
from jax.sharding import PartitionSpec as P

SPAN = 4
TIME_STEP = 0.5
TILE = 256
LANES = 128
HIGH = lax.Precision.HIGHEST
VMEM = pl.BlockSpec(memory_space=pltpu.VMEM)


def near_kernel(
    idx_hbm, low_ref, own_ref, high_ref, ops_ref, far_ref, mask_ref,
    out_ref, pad_ref, table, picked, idx_a, idx_b, sem,
):
    positions, coefs, width = ops_ref.shape
    leaves = own_ref.shape[0]
    tiles = leaves // TILE
    half = idx_a.shape[0] // TILE
    lag = 2

    def fetch_a(k):
        return pltpu.make_async_copy(idx_hbm.at[k, pl.ds(0, half * TILE)], idx_a, sem.at[0])

    def fetch_b(k):
        return pltpu.make_async_copy(
            idx_hbm.at[k, pl.ds(half * TILE, (positions - half) * TILE)], idx_b, sem.at[1]
        )

    fetch_a(0).start()
    fetch_b(0).start()
    for part, ref in enumerate((low_ref, own_ref, high_ref)):

        def fill(s, c, ref=ref, part=part):
            x = ref[pl.ds(pl.multiple_of(s * TILE, TILE), TILE), :].astype(jnp.float32)
            start = part * 2 * leaves + s * 2 * TILE
            table[pl.ds(start, TILE, stride=2), :] = x[:, :LANES]
            table[pl.ds(start + 1, TILE, stride=2), :] = x[:, LANES:]
            return c

        lax.fori_loop(0, leaves // TILE, fill, 0)
    pad_ref[pl.ds(640, 128), :] = jnp.zeros((128, leaves), jnp.bfloat16)

    def product(t):
        first = picked[t, pl.ds(0, TILE, stride=2), :].astype(jnp.bfloat16)
        second = picked[t, pl.ds(1, TILE, stride=2), :].astype(jnp.bfloat16)
        rows = jnp.concatenate([first, second], axis=1)[:, :width]
        return lax.dot_general(
            ops_ref[t], rows, (((1,), (1,)), ((), ())), preferred_element_type=jnp.float32
        )

    def tile_step(k, c):
        later = lax.min(k + 1, tiles - 1)
        total = None
        fetch_a(0).wait()
        for t in range(positions + lag):
            if t < positions:
                if t == half:
                    fetch_a(later).start()
                    fetch_b(0).wait()
                for i in range(TILE):
                    row = idx_a[t * TILE + i] if t < half else idx_b[(t - half) * TILE + i]
                    picked[t, pl.ds(2 * i, 2), :] = table[pl.ds(pl.multiple_of(row, 2), 2), :]
            if t >= lag:
                term = product(t - lag)
                total = term if total is None else total + term
        fetch_b(later).start()
        cols = pl.ds(pl.multiple_of(k * TILE, TILE), TILE)
        far = far_ref[...]
        value = total + jnp.concatenate([far] * (TILE // LANES), axis=1)
        value = (value * mask_ref[:, cols]).astype(jnp.bfloat16)
        out_ref[:, cols] = value
        pad_ref[pl.ds(0, coefs), cols] = value
        return c

    lax.fori_loop(0, tiles, tile_step, 0)
    fetch_a(0).wait()
    fetch_b(0).wait()


def near_call(idx, low, own, high, ops, far, mask):
    positions, coefs, _ = ops.shape
    leaves = own.shape[0]
    half = (positions + 1) // 2
    return pl.pallas_call(
        near_kernel,
        out_shape=(
            jax.ShapeDtypeStruct((coefs, leaves), jnp.bfloat16),
            jax.ShapeDtypeStruct((768, leaves), jnp.bfloat16),
        ),
        in_specs=[pl.BlockSpec(memory_space=pl.ANY)] + [VMEM] * 6,
        out_specs=(VMEM, VMEM),
        scratch_shapes=[
            pltpu.VMEM((6 * leaves, LANES), jnp.float32),
            pltpu.VMEM((positions, 2 * TILE, LANES), jnp.float32),
            pltpu.SMEM((half * TILE,), jnp.int32),
            pltpu.SMEM(((positions - half) * TILE,), jnp.int32),
            pltpu.SemaphoreType.DMA((2,)),
        ],
        compiler_params=pltpu.CompilerParams(vmem_limit_bytes=40 * 2**20),
        cost_estimate=pl.CostEstimate(
            flops=2 * positions * leaves * 256 * 664, bytes_accessed=20_000_000, transcendentals=0
        ),
        name="near",
    )(idx, low, own, high, ops, far, mask)


def base_kernel(conc_ref, dep_ref, cls_ref, shift_ref, out_ref):
    slots = conc_ref.shape[1]
    rows = lax.broadcasted_iota(jnp.int32, (slots, TILE), 0)
    pick = jnp.where(rows == dep_ref[...], 1.0, 0.0).astype(jnp.bfloat16)
    got = jnp.dot(conc_ref[...], pick, preferred_element_type=jnp.float32)
    kind = cls_ref[...]
    total = None
    for c in range(shift_ref.shape[0]):
        part = jnp.where(kind == c, got, 0.0).astype(jnp.bfloat16)
        term = jnp.dot(shift_ref[c], part, preferred_element_type=jnp.float32)
        total = term if total is None else total + term
    out_ref[...] = total.astype(jnp.bfloat16)


def base_call(conc, dep, cls, shift):
    width, slots = conc.shape
    return pl.pallas_call(
        base_kernel,
        out_shape=jax.ShapeDtypeStruct((width, slots), jnp.bfloat16),
        grid=(slots // TILE,),
        in_specs=[
            pl.BlockSpec(conc.shape, lambda s: (0, 0)),
            pl.BlockSpec((1, TILE), lambda s: (0, s)),
            pl.BlockSpec((1, TILE), lambda s: (0, s)),
            pl.BlockSpec(shift.shape, lambda s: (0, 0, 0)),
        ],
        out_specs=pl.BlockSpec((width, TILE), lambda s: (0, s)),
        compiler_params=pltpu.CompilerParams(vmem_limit_bytes=24 * 2**20),
        cost_estimate=pl.CostEstimate(
            flops=2 * slots * 256 * 4096, bytes_accessed=3_000_000, transcendentals=0
        ),
        name="base",
    )(conc, dep, cls, shift)


def send_kernel(slot_ref, vel_ref, out_ref):
    rows, leaves = out_ref.shape[0], vel_ref.shape[1]
    at = lax.broadcasted_iota(jnp.int32, (rows, leaves), 0) + pl.program_id(0) * rows
    pick = jnp.where(at == slot_ref[...], 1.0, 0.0).astype(jnp.bfloat16)
    out_ref[...] = lax.dot_general(
        pick, vel_ref[...], (((1,), (1,)), ((), ())), preferred_element_type=jnp.float32
    ).astype(jnp.bfloat16)


def send_call(slot, vel, slots):
    rows = 512
    return pl.pallas_call(
        send_kernel,
        out_shape=jax.ShapeDtypeStruct((slots, vel.shape[0]), jnp.bfloat16),
        grid=(slots // rows,),
        in_specs=[
            pl.BlockSpec(slot.shape, lambda s: (0, 0)),
            pl.BlockSpec(vel.shape, lambda s: (0, 0)),
        ],
        out_specs=pl.BlockSpec((rows, vel.shape[0]), lambda s: (s, 0)),
        compiler_params=pltpu.CompilerParams(vmem_limit_bytes=24 * 2**20),
        cost_estimate=pl.CostEstimate(
            flops=2 * slots * 1024 * 768, bytes_accessed=5_000_000, transcendentals=0
        ),
        name="send",
    )(slot, vel)


def advect_kernel(base_ref, got_ref, alive_ref, eval_ref, e0_ref, e1_ref, e2_ref, out_ref):
    nodes = out_ref.shape[1]
    values = lax.dot_general(
        base_ref[...], eval_ref[...], (((0,), (0,)), ((), ())), preferred_element_type=jnp.float32
    )
    got = got_ref[...]
    correction = None
    for j, (lo, hi, ref) in enumerate(((0, 256, e0_ref), (128, 512, e1_ref), (384, 768, e2_ref))):
        speed = jnp.dot(got[:, lo:hi], ref[...], preferred_element_type=jnp.float32)
        term = speed * values[:, (j + 1) * nodes : (j + 2) * nodes]
        correction = term if correction is None else correction + term
    result = alive_ref[...] * (values[:, :nodes] - TIME_STEP * correction)
    out_ref[...] = result.astype(jnp.bfloat16)


def advect_call(base, got, alive, evals, shifted):
    width, slots = base.shape
    nodes = evals.shape[1] // 4
    return pl.pallas_call(
        advect_kernel,
        out_shape=jax.ShapeDtypeStruct((slots, nodes), jnp.bfloat16),
        grid=(slots // TILE,),
        in_specs=[
            pl.BlockSpec((width, TILE), lambda s: (0, s)),
            pl.BlockSpec((TILE, got.shape[1]), lambda s: (s, 0)),
            pl.BlockSpec((TILE, 1), lambda s: (s, 0)),
            pl.BlockSpec(evals.shape, lambda s: (0, 0)),
        ]
        + [pl.BlockSpec(e.shape, lambda s: (0, 0)) for e in shifted],
        out_specs=pl.BlockSpec((TILE, nodes), lambda s: (s, 0)),
        compiler_params=pltpu.CompilerParams(vmem_limit_bytes=24 * 2**20),
        cost_estimate=pl.CostEstimate(
            flops=2 * slots * 256 * 2304, bytes_accessed=6_000_000, transcendentals=0
        ),
        name="advect",
    )(base, got, alive, evals, *shifted)


def local(
    density,
    vel_mask,
    near_list,
    near_ops,
    upward_ops,
    coupling_operators,
    coarse_weights,
    downward_ops,
    conc_owner,
    concentration,
    departure,
    departure_class,
    shift_ops,
    eval_ops,
):
    leaves, width = density.shape
    positions = near_list.shape[1]
    devices = lax.axis_size("leaf")
    me = lax.axis_index("leaf")
    box = me // SPAN
    slots = concentration.shape[0]
    capacity = slots // devices
    nodes = eval_ops.shape[1] // 4
    forward = [(i, i + 1) for i in range(devices - 1)]
    backward = [(i + 1, i) for i in range(devices - 1)]

    alive = vel_mask.astype(jnp.float32)
    live = (density.astype(jnp.float32) * alive[:, None]).astype(jnp.bfloat16)
    own = jnp.pad(live, ((0, 0), (0, 256 - width)))
    low = lax.ppermute(own, "leaf", forward)
    high = lax.ppermute(own, "leaf", backward)

    octant = (jnp.arange(leaves, dtype=jnp.int32)[:, None] % 8) == jnp.arange(8, dtype=jnp.int32)
    sums = jnp.dot(live.T, octant.astype(jnp.bfloat16), preferred_element_type=jnp.float32)
    part = jnp.einsum("po,opq->q", sums, upward_ops.astype(jnp.float32), precision=HIGH)

    owner = conc_owner[:, 0]
    named = (jnp.arange(devices, dtype=jnp.int32)[:, None] == owner[None, :]).astype(jnp.bfloat16)
    spot = jnp.arange(leaves, dtype=jnp.int32)
    before = (spot[:, None] < spot[None, :]).astype(jnp.bfloat16)
    count = jnp.dot(named, before, preferred_element_type=jnp.float32)
    rank = jnp.sum(count * named.astype(jnp.float32), axis=0).astype(jnp.int32)
    slot = (owner * capacity + rank)[None, :]
    ranked = (rank[:, None] == jnp.arange(capacity, dtype=jnp.int32)).astype(jnp.bfloat16)
    filled = jnp.dot(
        named, ranked * vel_mask[:, None].astype(jnp.bfloat16), preferred_element_type=jnp.float32
    )
    small = jnp.concatenate(
        [
            jnp.broadcast_to(jnp.pad(part, (0, 64 - part.shape[0]))[None, :], (devices, 64)),
            filled,
            jnp.zeros((devices, 64 - capacity), jnp.float32),
        ],
        axis=1,
    ).reshape(devices, 1, 128)
    small = lax.all_to_all(small, "leaf", split_axis=0, concat_axis=0, tiled=True)
    small = small.reshape(devices, 128)

    weight_row = jnp.repeat(lax.dynamic_slice_in_dim(coarse_weights, box, 1, 0), SPAN, axis=1)
    mixed = jnp.dot(weight_row, small[:, : part.shape[0]], precision=HIGH)
    expansion = jnp.dot(mixed, coupling_operators, precision=HIGH)
    far = jnp.einsum(
        "jq,oqp->jpo",
        expansion.reshape(3, -1),
        downward_ops.astype(jnp.float32),
        precision=HIGH,
    )
    far = jnp.tile(far.reshape(3 * width, 8), (1, 16))
    alive_slots = small[:, 64 : 64 + capacity].reshape(slots, 1)

    base = base_call(
        concentration.T,
        departure[None, :],
        departure_class[None, :],
        shift_ops.transpose(0, 2, 1),
    )

    rows = (near_list.T - me * leaves + leaves) * 2
    rows = rows.reshape(positions, leaves // TILE, TILE).transpose(1, 0, 2)
    rows = rows.reshape(leaves // TILE, positions * TILE)
    velocity, padded = near_call(
        rows, low, own, high, near_ops.transpose(0, 2, 1), far, alive[None, :]
    )
    send = send_call(slot, padded, slots)
    got = lax.all_to_all(
        send.reshape(devices, capacity, -1), "leaf", split_axis=0, concat_axis=0, tiled=True
    )
    first = eval_ops[:, :nodes]
    shifted = (
        jnp.pad(first, ((0, 256 - width), (0, 0))),
        jnp.pad(first, ((width - 128, 512 - 2 * width), (0, 0))),
        jnp.pad(first, ((2 * width - 384, 768 - 3 * width), (0, 0))),
    )
    advected = advect_call(base, got.reshape(slots, -1), alive_slots, eval_ops, shifted)
    return velocity.T, advected


def solution(mesh):
    placed = (
        P("leaf", None),
        P("leaf"),
        P("leaf", None),
        P(),
        P(),
        P(),
        P(),
        P(),
        P("leaf", None),
        P("leaf", None),
        P("leaf"),
        P("leaf"),
        P(),
        P(),
    )
    return jax.shard_map(
        local,
        mesh=mesh,
        in_specs=placed,
        out_specs=(P("leaf", None), P("leaf", None)),
        check_vma=False,
    )
```

time: 432 us -> 127 us (0.29)
  matrix products: 132 us -> 3.09 us
  local copies, waits for them, and re-layouts: 141 us -> 26.3 us
  blocking collectives: 67.2 us -> 0 us
  Pallas kernels: 0 us -> 45.6 us
  other arithmetic: 34.3 us -> 1.74 us
  starting transfers between devices: 26.1 us -> 21.7 us
    dot_general x42 -> x7, matrix products: 132 us -> 3.09 us  [the longest x1 1.22 us: local(): count = jnp.dot(named, before, preferred_element_type=jnp.float32)]
    gather x28 -> x0, local copies, waits for them, and re-layouts: 114 us -> none  [the longest x27 106 us: near_step(): picked = jnp.take(padded, rows, axis=0)]
    psum x1 -> x0, blocking collectives: 67.2 us -> none  [local(): moments = lax.psum(box_rows[:, None] * own_part[None, :], 'leaf')]
    pallas_call x0 -> x4, Pallas kernels: none -> 45.6 us  [the longest x1 26.2 us: near_call(): pl.pallas_call(near_kernel, out_shape=(jax.ShapeDtypeStruct((coefs, leave...]
    and x27 -> x0, other arithmetic: 21.3 us -> none  [near_step(): picked = jnp.take(padded, rows, axis=0)]
    unnamed x37 -> x42, local copies, waits for them, and re-layouts: 3.6 us -> 17.6 us
    dot_general x2 -> x0, local copies, waits for them, and re-layouts: 10.9 us -> none  [the longest x1 10.8 us: advect_rows(): jnp.dot(velocity_rows.reshape(-1, eval_ops.shape[0]), eval_ops[:, :nodes_...]
    convert_element_type x7 -> x3, other arithmetic: 8.8 us -> 0.98 us  [the longest x1 0.77 us: local(): vel_mask[:, None].astype(jnp.bfloat16)]
  transfers between devices with their start and end apart: 4 -> 4, of which waited for: 1 -> 2; matrix products, arithmetic and copies ran while one was open for 66% -> 12% of each run, Pallas kernels for 0% -> 8%
where the time goes in v1:
time: 127 us; the launch traced here: 126 us
  Pallas kernels  45.6 us (36%)
  waiting for transfers between devices  26.9 us (21%)
  local copies, waits for them, and re-layouts  26.3 us (21%)
  starting transfers between devices  21.7 us (17%)
  matrix products  3.09 us (2%)
  other arithmetic  1.74 us (1%)
    pallas_call x1, Pallas kernels, near_call(): pl.pallas_call(near_kernel, out_shape=(jax.ShapeDtypeStruct((coefs, leave...  26.2 us
    all_to_all x1, waiting for transfers between devices, local(): lax.all_to_all(send.reshape(devices, capacity, -1), 'leaf', split_axis=0,...  18.7 us
    unnamed x42, local copies, waits for them, and re-layouts  17.6 us
    all_to_all x1, starting transfers between devices, local(): lax.all_to_all(small, 'leaf', split_axis=0, concat_axis=0, tiled=True)  10.6 us
    pallas_call x1, Pallas kernels, base_call(): pl.pallas_call(base_kernel, out_shape=jax.ShapeDtypeStruct((width, slots)...  9.92 us
    all_to_all x1, waiting for transfers between devices, local(): lax.all_to_all(small, 'leaf', split_axis=0, concat_axis=0, tiled=True)  8.21 us
    pallas_call x1, Pallas kernels, advect_call(): pl.pallas_call(advect_kernel, out_shape=jax.ShapeDtypeStruct((slots, node...  5.32 us
    all_to_all x1, starting transfers between devices, local(): lax.all_to_all(send.reshape(devices, capacity, -1), 'leaf', split_axis=0,...  4.61 us
  transfers between devices with their start and end apart: 4, of which 2 were waited for; matrix products, arithmetic and copies ran while one was open for 12% of the time, Pallas kernels for 8%

profile of v1, /device:TPU:1, one launch (start us, length us, event | category | flops | bytes accessed | tf_op | source)
XLA Modules:
  0.0 126.3 jit_solution(9858055600472856654)
XLA Ops:
  1.4 1.2 copy.29
  3.0 4.5 %collective-permute-start = (bf16[1024,256]{1,0:T(8,128)(2,1)S(1)}, bf16[1024,256]{1,0:T(8,128)(2,1)S(1)}, u32[]{:S(2)}, u32[]{:S(2)}) collective-permute-start(bf16[1024,256]{1,0:T(8,128)(2,1)S(1)} %pad.20.own_ref), channel_id=1, source_target_pairs={{0,1},{1,2},{2,3},{3,4},{4,5},{5,6},{6,7},{7,8},{8,9},{9,10},{10,1... | collective-permute-start | bytes 1572872 | tf_op jit(solution)/shard_map/ppermute | solution.py:243
  7.5 1.9 %collective-permute-start.1 = (bf16[1024,256]{1,0:T(8,128)(2,1)S(1)}, bf16[1024,256]{1,0:T(8,128)(2,1)S(1)}, u32[]{:S(2)}, u32[]{:S(2)}) collective-permute-start(bf16[1024,256]{1,0:T(8,128)(2,1)S(1)} %pad.20.own_ref), channel_id=1, source_target_pairs={{1,0},{2,1},{3,2},{4,3},{5,4},{6,5},{7,6},{8,7},{9,8},{10,9},{11,1... | collective-permute-start | bytes 1572872 | tf_op jit(solution)/shard_map/ppermute | solution.py:244
  9.4 1.2 fusion.2
  12.7 10.6 %all-to-all-start = ((f32[128,1,128]{2,1,0:T(1,128)}), f32[128,1,128]{2,1,0:T(1,128)S(1)}, u32[]{:S(2)}, u32[]{:S(2)}) async-start(f32[128,1,128]{2,1,0:T(1,128)} %bitcast.7), calls=%async_computation | async-start | bytes 131072 | tf_op jit(solution)/shard_map/all_to_all | solution.py:269
  24.6 8.2 %all-to-all-done = f32[128,1,128]{2,1,0:T(1,128)S(1)} async-done(((f32[128,1,128]{2,1,0:T(1,128)}), f32[128,1,128]{2,1,0:T(1,128)S(1)}, u32[]{:S(2)}, u32[]{:S(2)}) %all-to-all-start) | async-done | bytes 65568 | tf_op jit(solution)/shard_map/all_to_all | solution.py:269
  33.9 3.6 %copy-done.7 = bf16[27,220,660]{1,2,0:T(8,128)(2,1)S(1)} copy-done((bf16[27,220,660]{1,2,0:T(8,128)(2,1)S(1)}, bf16[27,220,660]{1,2,0:T(8,128)(2,1)}, u32[]{:S(2)}) %copy-start.7) | copy-done | bytes 7840824
  37.5 26.2 %near.1 = (bf16[660,1024]{1,0:T(8,128)(2,1)}, bf16[768,1024]{1,0:T(8,128)(2,1)S(1)}) custom-call(s32[4,6912]{1,0:T(4,128)S(1)} %bitcast.54, bf16[1024,256]{1,0:T(8,128)(2,1)S(1)} %collective-permute-done.low_ref, bf16[1024,256]{1,0:T(8,128)(2,1)S(1)} %pad.20.own_ref, bf16[1024,256]{1,0:T(8,128)(2,1)S(1)} %collective-permute-done.1.high_ref, ...), custom_call_target="tpu_custom_call" | custom-call | flops 9399435264 | bytes 20000000 | tf_op jit(solution)/shard_map/near/pallas_call | solution.py:89
  63.7 4.1 %send.1 = bf16[2048,768]{1,0:T(8,128)(2,1)S(1)} custom-call(s32[1,1024]{1,0:T(1,128)S(1)} %bitcast_add_fusion.slot_ref, bf16[768,1024]{1,0:T(8,128)(2,1)S(1)} %get-tuple-element.5.vel_ref), custom_call_target="tpu_custom_call" | custom-call | flops 3221225472 | bytes 5000000 | tf_op jit(solution)/shard_map/send/pallas_call | solution.py:158
  67.8 1.6 %copy-done.1 = bf16[2048,768]{1,0:T(8,128)(2,1)} copy-done((bf16[2048,768]{1,0:T(8,128)(2,1)}, bf16[2048,768]{1,0:T(8,128)(2,1)S(1)}, u32[]{:S(2)}) %copy-start.1) | copy-done | bytes 3145752
  69.4 4.6 %all-to-all-start.1 = ((bf16[128,16,768]{2,1,0:T(8,128)(2,1)}), bf16[128,16,768]{2,1,0:T(8,128)(2,1)S(1)}, u32[]{:S(2)}, u32[]{:S(2)}) async-start(bf16[128,16,768]{2,1,0:T(8,128)(2,1)} %bitcast.52), calls=%async_computation.1 | async-start | bytes 6291456 | tf_op jit(solution)/shard_map/all_to_all | solution.py:298
  74.0 1.5 %slice.11 = bf16[220,256]{1,0:T(8,128)(2,1)} slice(bf16[220,1024]{1,0:T(8,128)(2,1)} %eval_ref.1), slice={[0:220], [0:256]} | slice | bytes 225280 | tf_op jit(solution)/shard_map/slice | solution.py:301
  76.5 2.3 %copy.33 = bf16[8,220,220]{1,2,0:T(8,128)(2,1)} copy(bf16[8,220,220]{2,0,1:T(8,128)(2,1)} %param.26) | data formatting | bytes 1548800 | tf_op args[12]
  78.9 1.8 %fusion.21 = (bf16[384,256]{1,0:T(8,128)(2,1)}, bf16[384,256]{1,0:T(8,128)(2,1)}) fusion(bf16[220,256]{1,0:T(8,128)(2,1)} %slice.11), kind=kLoop, calls=%fused_computation.38 | loop fusion | bytes 505856 | tf_op jit(solution)/shard_map/jit(_pad)/pad | solution.py:305
  80.6 1.2 copy-done.3
  81.8 1.2 copy-done.8
  83.0 9.9 %base.1.base_ref = bf16[220,2048]{1,0:T(8,128)(2,1)S(1)} custom-call(bf16[220,2048]{1,0:T(8,128)(2,1)S(1)} %bitcast.57, s32[1,2048]{1,0:T(1,128)S(1)} %bitcast.58, s32[1,2048]{1,0:T(1,128)S(1)} %bitcast.59, bf16[8,220,220]{2,1,0:T(8,128)(2,1)S(1)} %bitcast.53), custom_call_target="tpu_custom_call" | custom-call | flops 4294967296 | bytes 3000000 | tf_op jit(solution)/shard_map/base/pallas_call | solution.py:128
  92.9 0.9 copy-done.11
  94.6 2.4 %reshape.102.alive_ref = f32[2048,1]{1,0:T(8,128)} reshape(f32[128,16]{1,0:T(8,128)} %slice.13) | data formatting | bytes 16384 | tf_op jit(solution)/shard_map/reshape | solution.py:282
  97.0 18.7 %all-to-all-done.1 = bf16[128,16,768]{2,1,0:T(8,128)(2,1)S(1)} async-done(((bf16[128,16,768]{2,1,0:T(8,128)(2,1)}), bf16[128,16,768]{2,1,0:T(8,128)(2,1)S(1)}, u32[]{:S(2)}, u32[]{:S(2)}) %all-to-all-start.1) | async-done | bytes 3145760 | tf_op jit(solution)/shard_map/all_to_all | solution.py:298
  115.7 1.2 copy-done.2
  118.7 1.0 copy-done.6
  119.8 1.2 copy-done.12
  120.9 5.3 %advect.1 = bf16[2048,256]{1,0:T(8,128)(2,1)} custom-call(bf16[220,2048]{1,0:T(8,128)(2,1)S(1)} %copy-done.12, bf16[2048,768]{1,0:T(8,128)(2,1)S(1)} %bitcast.51, f32[2048,1]{1,0:T(8,128)S(1)} %copy-done.2, bf16[220,1024]{1,0:T(8,128)(2,1)S(1)} %copy-done.6, bf16[256,256]{1,0:T(8,128)(2,1)S(1)} %pad.22.e0_ref, bf16[384,256]{1,0:T(8,128)(2,1)S(1)} %copy-done.5, ...), custom_call_target="tpu_custom_call" | custom-call | flops 2415919104 | bytes 6000000 | tf_op jit(solution)/shard_map/advect/pallas_call | solution.py:193
  (61 shorter events, 8.7 us)
Async XLA Ops:
  0.6 32.7 %copy-start = (bf16[8,56,220]{2,1,0:T(8,128)(2,1)S(1)}, bf16[8,56,220]{2,1,0:T(8,128)(2,1)}, u32[]{:S(2)}) copy-start(bf16[8,56,220]{2,1,0:T(8,128)(2,1)} %param.21) | copy-start | bytes 591364
  0.6 10.4 %copy-start.18 = (bf16[8,220,56]{1,2,0:T(8,128)(2,1)S(1)}, bf16[8,220,56]{1,2,0:T(8,128)(2,1)}, u32[]{:S(2)}) copy-start(bf16[8,220,56]{1,2,0:T(8,128)(2,1)} %param.18) | copy-start | bytes 591364
  1.4 10.0 %copy-start.17 = (s32[1024,1]{0,1:T(1,128)S(1)}, s32[1024,1]{0,1:T(1,128)}, u32[]{:S(2)}) copy-start(s32[1024,1]{0,1:T(1,128)} %param.22) | copy-start | bytes 12292
  2.7 20.7 %copy-start.15 = (s32[1024,27]{0,1:T(8,128)S(1)}, s32[1024,27]{0,1:T(8,128)}, u32[]{:S(2)}) copy-start(s32[1024,27]{0,1:T(8,128)} %param.16) | copy-start | bytes 331780
  2.7 21.6 %copy-start.16 = (f32[56,168]{1,0:T(8,128)S(1)}, f32[56,168]{1,0:T(8,128)}, u32[]{:S(2)}) copy-start(f32[56,168]{1,0:T(8,128)} %param.19) | copy-start | bytes 112900
  3.0 30.8 %collective-permute-start = (bf16[1024,256]{1,0:T(8,128)(2,1)S(1)}, bf16[1024,256]{1,0:T(8,128)(2,1)S(1)}, u32[]{:S(2)}, u32[]{:S(2)}) collective-permute-start(bf16[1024,256]{1,0:T(8,128)(2,1)S(1)} %pad.20.own_ref), channel_id=1, source_target_pairs={{0,1},{1,2},{2,3},{3,4},{4,5},{5,6},{6,7},{7,8},{8,9},{9,10},{10,1... | collective-permute-start | bytes 1572872 | tf_op jit(solution)/shard_map/ppermute | solution.py:243
  7.5 26.3 %collective-permute-start.1 = (bf16[1024,256]{1,0:T(8,128)(2,1)S(1)}, bf16[1024,256]{1,0:T(8,128)(2,1)S(1)}, u32[]{:S(2)}, u32[]{:S(2)}) collective-permute-start(bf16[1024,256]{1,0:T(8,128)(2,1)S(1)} %pad.20.own_ref), channel_id=1, source_target_pairs={{1,0},{2,1},{3,2},{4,3},{5,4},{6,5},{7,6},{8,7},{9,8},{10,9},{11,1... | collective-permute-start | bytes 1572872 | tf_op jit(solution)/shard_map/ppermute | solution.py:244
  12.7 20.1 %all-to-all-start = ((f32[128,1,128]{2,1,0:T(1,128)}), f32[128,1,128]{2,1,0:T(1,128)S(1)}, u32[]{:S(2)}, u32[]{:S(2)}) async-start(f32[128,1,128]{2,1,0:T(1,128)} %bitcast.7), calls=%async_computation | async-start | bytes 131072 | tf_op jit(solution)/shard_map/all_to_all | solution.py:269
  32.8 0.8 copy-start.13
  33.8 3.6 %copy-start.7 = (bf16[27,220,660]{1,2,0:T(8,128)(2,1)S(1)}, bf16[27,220,660]{1,2,0:T(8,128)(2,1)}, u32[]{:S(2)}) copy-start(bf16[27,220,660]{1,2,0:T(8,128)(2,1)} %param.17) | copy-start | bytes 23522404
  67.8 1.6 %copy-start.1 = (bf16[2048,768]{1,0:T(8,128)(2,1)}, bf16[2048,768]{1,0:T(8,128)(2,1)S(1)}, u32[]{:S(2)}) copy-start(bf16[2048,768]{1,0:T(8,128)(2,1)S(1)} %send.1) | copy-start | bytes 9437188
  69.4 11.2 %copy-start.9 = (s32[2048]{0:T(1024)S(1)}, s32[2048]{0:T(1024)}, u32[]{:S(2)}) copy-start(s32[2048]{0:T(1024)} %param.24) | copy-start | bytes 24580
  69.4 11.2 %copy-start.10 = (s32[2048]{0:T(1024)S(1)}, s32[2048]{0:T(1024)}, u32[]{:S(2)}) copy-start(s32[2048]{0:T(1024)} %param.25) | copy-start | bytes 24580
  69.4 46.2 %all-to-all-start.1 = ((bf16[128,16,768]{2,1,0:T(8,128)(2,1)}), bf16[128,16,768]{2,1,0:T(8,128)(2,1)S(1)}, u32[]{:S(2)}, u32[]{:S(2)}) async-start(bf16[128,16,768]{2,1,0:T(8,128)(2,1)} %bitcast.52), calls=%async_computation.1 | async-start | bytes 6291456 | tf_op jit(solution)/shard_map/all_to_all | solution.py:298
  80.6 1.2 copy-start.3
  81.8 1.2 copy-start.8
  83.0 10.9 %copy-start.14 = (f32[128,1,128]{2,1,0:T(1,128)S(1)}, f32[128,1,128]{2,1,0:T(1,128)}, u32[]{:S(2)}) copy-start(f32[128,1,128]{2,1,0:T(1,128)} %copy-done.13) | copy-start | bytes 196612
  92.9 0.9 copy-start.11
  115.7 1.2 copy-start.2
  116.9 0.9 copy-start.4
  117.8 0.9 copy-start.5
  118.7 1.0 copy-start.6
  119.8 1.2 copy-start.12
